TPU v7x, 32 devices: a whole 2x2x4 slice. The times are simulated.
32 devices in a mesh: groups: 2 (over x), tm: 16 (over z, y, core).
Axes of the slice: x: 2, y: 2, z: 4, core: 2. Of those that a mesh axis runs over, the one named last changes fastest.
Arguments:
- queries: bfloat16 [6144, 2560], P(('groups', 'tm')), parts along dimension 0, may hold values from -6 to 6
- keys: bfloat16 [6144, 2560], P(('groups', 'tm')), parts along dimension 0, may hold values from -6 to 6
- values: bfloat16 [6144, 2560], P(('groups', 'tm')), parts along dimension 0, may hold values from -6 to 6
- q_gain: float32 [2560], replicated, may hold values from 0.5 to 1.5
- k_gain: float32 [2560], replicated, may hold values from 0.5 to 1.5
- out_weight: bfloat16 [2560, 5120], P('tm'), may hold values from -0.125 to 0.125
- out_gate: float32 [5120], replicated, may hold values from 0.5 to 2
- reach: int32 [32, 2], P(('groups', 'tm')), parts along dimension 0, may hold values from 0 to 1
Outputs:
- mixed: bfloat16 [6144, 5120], P(('groups', 'tm')), parts along dimension 0
There are 2 independent parts, one for each index of `groups`. A program takes and returns all parts, laid end to end along the dimension named above; an argument that names none is the same for every part. Nothing has to cross between parts.
Inputs may be any that keep to these rules, and one draw needn't show every extreme that they name: `reach`: requests past the first or last tile are ignored.
All inputs are finite; a program needn't handle non-finite values.
Results may differ from a plain program's by a relative error of at most 0.0076.
Values may be sent and summed in bfloat16 or wider, within the bound.
A program may use at most 128 MiB of HBM per device.

v0:
```python
import jax
import jax.numpy as jnp
from jax import lax
from jax.sharding import PartitionSpec as P

HD = 128
TT = 4
TH = 6
TW = 8


def shifted(shard, axis, by):
    peers = lax.axis_size(axis)
    pairs = [(i, i + by) for i in range(peers) if 0 <= i + by < peers]
    return lax.ppermute(shard, axis, pairs)


def rms_scaled(block, gain):
    values32 = block.astype(jnp.float32)
    inverse = lax.rsqrt(jnp.mean(values32 * values32, axis=-1, keepdims=True) + 1e-06)
    return (values32 * inverse * gain).astype(jnp.bfloat16)


def local(queries, keys, values, q_gain, k_gain, out_weight, out_gate, reach):
    tile = TT * TH * TW
    rows = queries.shape[0]
    chans = queries.shape[1]
    heads = chans // HD
    count = rows // tile
    scale = HD ** (-0.5)
    q_norm = rms_scaled(queries, q_gain)
    k_norm = rms_scaled(keys, k_gain)
    before_k, before_v = shifted((k_norm, values), "tm", 1)
    after_k, after_v = shifted((k_norm, values), "tm", -1)
    key_buffer = jnp.concatenate([before_k, k_norm, after_k], axis=0).reshape(
        count + 2, tile, heads, HD
    )
    val_buffer = jnp.concatenate([before_v, values, after_v], axis=0).reshape(
        count + 2, tile, heads, HD
    )
    position = lax.axis_index("tm")
    first_tile = position * count
    total_tiles = lax.axis_size("tm") * count
    global_tile = first_tile + jnp.arange(count, dtype=jnp.int32)
    valid = jnp.stack(
        [
            (reach[:, 0] == 1) & (global_tile > 0),
            global_tile >= 0,
            (reach[:, 1] == 1) & (global_tile < total_tiles - 1),
        ],
        axis=1,
    )
    query_tiles = q_norm.reshape(count, tile, heads, HD)
    seen_k = jnp.stack([key_buffer[offset : offset + count] for offset in range(3)], axis=1)
    seen_v = jnp.stack([val_buffer[offset : offset + count] for offset in range(3)], axis=1)
    logits = (
        jnp.einsum("nqhd,nokhd->nhqok", query_tiles, seen_k, preferred_element_type=jnp.float32)
        * scale
    )
    logits = jnp.where(valid[:, None, None, :, None], logits, -1e30)
    logits = logits.reshape(count, heads, tile, 3 * tile)
    top = jnp.max(logits, axis=-1, keepdims=True)
    expo = jnp.exp(logits - top)
    weights = (expo / jnp.sum(expo, axis=-1, keepdims=True)).astype(jnp.bfloat16)
    attended = jnp.einsum(
        "nhqk,nkhd->nqhd",
        weights,
        seen_v.reshape(count, 3 * tile, heads, HD),
        preferred_element_type=jnp.float32,
    ).astype(jnp.bfloat16)
    attended = attended.reshape(rows, chans)
    full_weight = lax.all_gather(out_weight, "tm", axis=0, tiled=True)
    projected = jnp.dot(attended, full_weight, preferred_element_type=jnp.float32)
    return (out_gate * projected).astype(jnp.bfloat16)


def solution(mesh):
    return jax.shard_map(
        local,
        mesh=mesh,
        in_specs=(
            P(("groups", "tm"), None),
            P(("groups", "tm"), None),
            P(("groups", "tm"), None),
            P(),
            P(),
            P("tm", None),
            P(),
            P(("groups", "tm"), None),
        ),
        out_specs=P(("groups", "tm"), None),
        check_vma=False,
    )
```

profile of v0, /device:TPU:4, one launch (start us, length us, event | category | flops | bytes accessed | tf_op | source)
XLA Modules:
  0.0 201.3 jit_solution(11805782908131688679)
XLA Ops:
  6.5 0.0 all-gather.2.cloned.1.call-start
  6.5 0.7 all-gather.2.cloned.1.call-update
  7.3 1.5 fusion.5
  8.7 0.0 copy-done.1
  8.8 0.0 copy-start.6
  8.8 1.0 fusion.7
  9.8 1.9 collective-permute-start.2
  11.7 3.6 %collective-permute-start.3 = (bf16[192,2560]{1,0:T(8,128)(2,1)S(1)}, bf16[192,2560]{1,0:T(8,128)(2,1)}, u32[]{:S(2)}, u32[]{:S(2)}) collective-permute-start(bf16[192,2560]{1,0:T(8,128)(2,1)S(1)} %fusion.7), channel_id=1, source_target_pairs={{1,0},{2,1},{3,2},{4,3},{5,4},{6,5},{7,6},{8,7},{9,8},{10,9},{11,1... | collective-permute-start | bytes 2949128 | tf_op jit(solution)/shard_map/ppermute | solution.py:15
  15.4 1.9 collective-permute-start
  17.3 3.6 %collective-permute-start.1 = (bf16[192,2560]{1,0:T(8,128)(2,1)}, bf16[192,2560]{1,0:T(8,128)(2,1)}, u32[]{:S(2)}, u32[]{:S(2)}) collective-permute-start(bf16[192,2560]{1,0:T(8,128)(2,1)} %param.10), channel_id=1, source_target_pairs={{1,0},{2,1},{3,2},{4,3},{5,4},{6,5},{7,6},{8,7},{9,8},{10,9},{11,1... | collective-permute-start | bytes 2949128 | tf_op jit(solution)/shard_map/ppermute | solution.py:15
  20.9 0.7 stack.45
  21.6 1.7 stack.37
  23.3 0.0 copy-done.6
  23.3 0.6 fusion.17
  25.2 1.2 copy.16
  26.4 0.1 add_bitcast_fusion
  26.5 1.5 fusion.2
  27.9 23.3 %collective-permute-done.2 = bf16[192,2560]{1,0:T(8,128)(2,1)} collective-permute-done((bf16[192,2560]{1,0:T(8,128)(2,1)S(1)}, bf16[192,2560]{1,0:T(8,128)(2,1)}, u32[]{:S(2)}, u32[]{:S(2)}) %collective-permute-start.2) | collective-permute-done | bytes 983072 | tf_op jit(solution)/shard_map/ppermute | solution.py:15
  51.3 1.7 stack.44
  53.0 1.2 copy.15
  54.1 0.0 collective-permute-done.3
  54.1 1.7 stack.46
  55.9 0.2 copy.17
  56.1 0.0 copy-done.3
  56.1 0.0 copy-start.2
  56.1 0.0 copy-start.5
  56.1 1.6 pad_maximum_fusion.1
  57.7 0.0 copy-done.2
  57.7 0.0 copy-done.5
  57.7 6.1 %fusion.13 = f32[20,192,576]{1,2,0} fusion(bf16[20,128,576]{1,2,0:T(8,128)(2,1)S(1)} %bitcast.38, bf16[192,2560]{1,0:T(8,128)(2,1)S(1)} %copy-done.2, f32[2560]{0:T(1024)S(1)} %copy-done.5, f32[192]{0:T(256)S(1)} %add_rsqrt_fusion.1), kind=kOutput, calls=%fused_computation.23 | convolution fusion | flops 568197120 | bytes 12790528
  63.8 12.2 %fusion.16 = (f32[20,192]{1,0:T(8,128)}, f32[20,192,3,192]{1,3,2,0:T(8,128)}) fusion(f32[20,192,3,192]{1,3,2,0:T(8,128)} %bitcast.37, pred[3]{0:T(512)(128)(4,1)S(1)} %add_bitcast_fusion), kind=kLoop, calls=%fused_computation.29 | loop fusion | flops 6631680 | bytes 17710084 | tf_op jit(solution)/shard_map/reduce_max | solution.py:62
  76.0 11.7 %copy.19 = f32[20,192,576]{2,1,0:T(8,128)} copy(f32[20,192,576]{1,2,0:T(8,128)} %bitcast.36) | data formatting | bytes 17694720 | tf_op jit(solution)/shard_map/reshape | solution.py:61
  87.8 5.5 %collective-permute-done = bf16[192,2560]{1,0:T(8,128)(2,1)} collective-permute-done((bf16[192,2560]{1,0:T(8,128)(2,1)}, bf16[192,2560]{1,0:T(8,128)(2,1)}, u32[]{:S(2)}, u32[]{:S(2)}) %collective-permute-start) | collective-permute-done | bytes 983072 | tf_op jit(solution)/shard_map/ppermute | solution.py:15
  93.2 1.7 stack.36
  94.9 0.0 collective-permute-done.1
  94.9 1.7 stack.38
  96.6 0.0 copy-start
  96.6 0.6 pad_maximum_fusion
  97.3 0.0 copy-start.4
  97.3 0.7 copy.14
  98.0 3.2 %copy-done = f32[20,192,3,192]{1,3,2,0:T(8,128)S(1)} copy-done((f32[20,192,3,192]{1,3,2,0:T(8,128)S(1)}, f32[20,192,3,192]{1,3,2,0:T(8,128)}, u32[]{:S(2)}) %copy-start) | copy-done | bytes 8847384
  101.2 1.8 exponential_reduce_fusion
  103.0 0.0 copy-start.7
  103.0 5.4 %fusion.9 = bf16[1,192,20,128]{3,1,2,0:T(8,128)(2,1)S(1)} fusion(bf16[576,20,128]{2,0,1:T(8,128)(2,1)S(1)} %bitcast.39, f32[20,192,576]{2,1,0:T(8,128)} %copy.19, f32[20,192]{1,0:T(8,128)S(1)} %exponential_reduce_fusion, f32[20,192]{1,0:T(8,128)S(1)} %copy-done.4), kind=kOutput, calls=%fused_computation.19 | convolution fusion | flops 573358080 | bytes 12810240 | tf_op jit(solution)/shard_map/nhqk,nkhd->nqhd/dot_general | solution.py:65
  108.4 0.7 copy.20
  109.1 72.7 %all-gather.2.cloned.1.call-done = bf16[2560,5120]{1,0:T(8,128)(2,1)} async-done(((bf16[160,5120]{1,0:T(8,128)(2,1)}), bf16[2560,5120]{1,0:T(8,128)(2,1)}) %all-gather.2.cloned.1.call-update) | async-done | bytes 26214416 | tf_op jit(solution)/shard_map/all_gather | solution.py:72
  181.7 0.0 copy-done.7
  181.7 12.7 %fusion = bf16[192,5120]{1,0:T(8,128)(2,1)} fusion(bf16[2560,5120]{1,0:T(8,128)(2,1)} %all-gather.2.cloned.1.call-done, f32[5120]{0:T(1024)S(1)} %copy-done.7, bf16[24,8,20,128]{3,2,1,0:T(8,128)(2,1)S(1)} %bitcast.40), kind=kOutput, calls=%fused_computation.4 | convolution fusion | flops 5035130880 | bytes 29184000 | tf_op jit(solution)/shard_map/dot_general | solution.py:73
  (5 shorter events, 0.0 us)
Async XLA Ops:
  6.5 2.2 %copy-start.1 = (bf16[192,2560]{1,0:T(8,128)(2,1)S(1)}, bf16[192,2560]{1,0:T(8,128)(2,1)}, u32[]{:S(2)}) copy-start(bf16[192,2560]{1,0:T(8,128)(2,1)} %param.9) | copy-start | bytes 2949124
  6.5 175.2 %all-gather.2.cloned.1.call-start = ((), (), s32[]{:S(2)}) async-start(), calls=%async_computation | async-start | bytes 27852800 | tf_op jit(solution)/shard_map/all_gather | solution.py:72
  8.8 14.5 %copy-start.6 = (s32[1,2]{1,0:T(1,128)S(1)}, s32[1,2]{1,0:T(1,128)}, u32[]{:S(2)}) copy-start(s32[1,2]{1,0:T(1,128)} %param.15) | copy-start | bytes 28
  9.8 41.5 %collective-permute-start.2 = (bf16[192,2560]{1,0:T(8,128)(2,1)S(1)}, bf16[192,2560]{1,0:T(8,128)(2,1)}, u32[]{:S(2)}, u32[]{:S(2)}) collective-permute-start(bf16[192,2560]{1,0:T(8,128)(2,1)S(1)} %fusion.7), channel_id=1, source_target_pairs={{0,1},{1,2},{2,3},{3,4},{4,5},{5,6},{6,7},{7,8},{8,9},{9,10},{10,1... | collective-permute-start | bytes 2949128 | tf_op jit(solution)/shard_map/ppermute | solution.py:15
  11.7 42.4 %collective-permute-start.3 = (bf16[192,2560]{1,0:T(8,128)(2,1)S(1)}, bf16[192,2560]{1,0:T(8,128)(2,1)}, u32[]{:S(2)}, u32[]{:S(2)}) collective-permute-start(bf16[192,2560]{1,0:T(8,128)(2,1)S(1)} %fusion.7), channel_id=1, source_target_pairs={{1,0},{2,1},{3,2},{4,3},{5,4},{6,5},{7,6},{8,7},{9,8},{10,9},{11,1... | collective-permute-start | bytes 2949128 | tf_op jit(solution)/shard_map/ppermute | solution.py:15
  15.4 77.9 %collective-permute-start = (bf16[192,2560]{1,0:T(8,128)(2,1)}, bf16[192,2560]{1,0:T(8,128)(2,1)}, u32[]{:S(2)}, u32[]{:S(2)}) collective-permute-start(bf16[192,2560]{1,0:T(8,128)(2,1)} %param.10), channel_id=1, source_target_pairs={{0,1},{1,2},{2,3},{3,4},{4,5},{5,6},{6,7},{7,8},{8,9},{9,10},{10,1... | collective-permute-start | bytes 2949128 | tf_op jit(solution)/shard_map/ppermute | solution.py:15
  17.3 77.6 %collective-permute-start.1 = (bf16[192,2560]{1,0:T(8,128)(2,1)}, bf16[192,2560]{1,0:T(8,128)(2,1)}, u32[]{:S(2)}, u32[]{:S(2)}) collective-permute-start(bf16[192,2560]{1,0:T(8,128)(2,1)} %param.10), channel_id=1, source_target_pairs={{1,0},{2,1},{3,2},{4,3},{5,4},{6,5},{7,6},{8,7},{9,8},{10,9},{11,1... | collective-permute-start | bytes 2949128 | tf_op jit(solution)/shard_map/ppermute | solution.py:15
  54.1 2.0 copy-start.3
  56.1 1.6 copy-start.2
  56.1 1.6 copy-start.5
  96.6 4.6 %copy-start = (f32[20,192,3,192]{1,3,2,0:T(8,128)S(1)}, f32[20,192,3,192]{1,3,2,0:T(8,128)}, u32[]{:S(2)}) copy-start(f32[20,192,3,192]{1,3,2,0:T(8,128)} %get-tuple-element.6) | copy-start | bytes 26542084
  97.3 4.0 %copy-start.4 = (f32[20,192]{1,0:T(8,128)S(1)}, f32[20,192]{1,0:T(8,128)}, u32[]{:S(2)}) copy-start(f32[20,192]{1,0:T(8,128)} %get-tuple-element.5) | copy-start | bytes 46084
  103.0 78.7 %copy-start.7 = (f32[5120]{0:T(1024)S(1)}, f32[5120]{0:T(1024)}, u32[]{:S(2)}) copy-start(f32[5120]{0:T(1024)} %param.14) | copy-start | bytes 61444
Sparse Core Ops, SparseCore 0:
  8.9 172.7 all-gather.1
where the time goes:
time: 203 us; the launch traced here: 201 us
  waiting for transfers between devices  102 us (50%)
  local copies, waits for them, and re-layouts  28.6 us (14%)
  matrix products  24.2 us (12%)
  other arithmetic  20.3 us (10%)
  between operations  14.9 us (7%)
  starting transfers between devices  11.1 us (5%)
    all_gather x1, waiting for transfers between devices, local(): full_weight = lax.all_gather(out_weight, 'tm', axis=0, tiled=True)  72.7 us
    ppermute x4, waiting for transfers between devices, shifted(): return lax.ppermute(shard, axis, pairs)  28.8 us
    dot_general x1, matrix products, local(): jnp.dot(attended, full_weight, preferred_element_type=jnp.float32)  12.7 us
    reduce_max x1, other arithmetic, local(): top = jnp.max(logits, axis=-1, keepdims=True)  12.2 us
    reshape x1, local copies, waits for them, and re-layouts, local(): logits = logits.reshape(count, heads, tile, 3 * tile)  11.7 us
    ppermute x4, starting transfers between devices, shifted(): return lax.ppermute(shard, axis, pairs)  11.1 us
    another operation x6, local copies, waits for them, and re-layouts, local(): jnp.stack([key_buffer[offset:offset + count] for offset in range(3)], axi...  6.58 us
    unnamed x1, matrix products  6.06 us
  transfers between devices with their start and end apart: 5, of which 3 were waited for; matrix products, arithmetic and copies ran while one was open for 28% of the time, Pallas kernels for 0%

commit v1 on v0

--- a/solution.py
+++ b/solution.py
@@ -1,12 +1,17 @@
+import functools
+
 import jax
 import jax.numpy as jnp
 from jax import lax
+from jax.experimental import pallas as pl
+from jax.experimental.pallas import tpu as pltpu
 from jax.sharding import PartitionSpec as P
 
 HD = 128
 TT = 4
 TH = 6
 TW = 8
+MESH = pl.DeviceIdType.MESH
 
 
 def shifted(shard, axis, by):
@@ -74,9 +79,369 @@
     return (out_gate * projected).astype(jnp.bfloat16)
 
 
+def lane_pieces(half):
+    lanes = half // 256
+    last = max(lanes // 5, 1)
+    first = (lanes - last + 1) // 2
+    widths = [w * 128 for w in (first, lanes - last - first, last) if w > 0]
+    offsets, at = [], 0
+    for w in widths:
+        offsets.append(at)
+        at += 2 * w
+    return list(zip(offsets, widths))
+
+
+def fused_kernel(
+    ring, q_ref, k_ref, v_ref, qg_ref, kg_ref, w_ref, gate_ref, reach_ref, o_ref,
+    wbuf, kbuf, vbuf, qn, att, sbuf,
+    ring_ss, ring_rs, chip_ss, chip_rs, own_ss, own_rs, halo_ss, halo_rs,
+    att_ss, att_rs, out_ss, out_rs, local_sem,
+):
+    rows, chans = q_ref.shape
+    depth, wide = w_ref.shape
+    half = wide // 2
+    heads = chans // HD
+    pieces = lane_pieces(half)
+    far = ring // 2
+    tiles = 2 * ring
+    g, t = lax.axis_index("groups"), lax.axis_index("tm")
+    core, chip = t % 2, t // 2
+    row, col = chip // 2, chip % 2
+    pos = row * (1 - col) + (ring - 1 - row) * col
+    col0 = (g % 2) * half
+
+    def chip_at(place):
+        back = place // far
+        line = place * (1 - back) + (ring - 1 - place) * back
+        return 2 * line + back
+
+    def peer(group, tm):
+        return (group, tm)
+
+    nxt = peer(g, 2 * chip_at((pos + 1) % ring) + core)
+    prv = peer(g, 2 * chip_at((pos + ring - 1) % ring) + core)
+    mate = peer(g, 2 * chip + 1 - core)
+    cross = peer(g + 1 - 2 * (g % 2), t)
+    outside = t - 1 + 2 * core
+    has_outside = (outside >= 0) & (outside < tiles)
+
+    def remote(src, dst, ss, rs, dev):
+        return pltpu.make_async_remote_copy(
+            src_ref=src, dst_ref=dst, send_sem=ss, recv_sem=rs, device_id=dev, device_id_type=MESH
+        )
+
+    barrier = pltpu.get_barrier_semaphore()
+    for dev in (nxt, prv, mate, cross):
+        pl.semaphore_signal(barrier, inc=1, device_id=dev, device_id_type=MESH)
+
+    @pl.when(has_outside)
+    def _():
+        pl.semaphore_signal(barrier, inc=1, device_id=peer(g, outside), device_id_type=MESH)
+        pl.semaphore_wait(barrier, 5)
+
+    @pl.when(jnp.logical_not(has_outside))
+    def _():
+        pl.semaphore_wait(barrier, 4)
+
+    def halo(side):
+        to = peer(g, t + (1 if side else -1))
+        there = pl.ds((0 if side else 2) * rows, rows)
+        return [
+            remote(k_ref, kbuf.at[there], halo_ss.at[side, 0], halo_rs.at[side, 0], to),
+            remote(v_ref, vbuf.at[there], halo_ss.at[side, 1], halo_rs.at[side, 1], to),
+        ]
+
+    not_first, not_last = t > 0, t < tiles - 1
+
+    @pl.when(not_last)
+    def _():
+        for c in halo(1):
+            c.start()
+
+    @pl.when(not_first)
+    def _():
+        for c in halo(0):
+            c.start()
+
+    own_rows = pl.ds(pl.multiple_of(t * depth, 16), depth)
+    own_cols = pl.ds(pl.multiple_of(col0, 128), half)
+    local_w = pltpu.make_async_copy(w_ref.at[:, own_cols], wbuf.at[own_rows], local_sem.at[0])
+    local_v = pltpu.make_async_copy(v_ref, vbuf.at[pl.ds(rows, rows)], local_sem.at[1])
+    local_w.start()
+    local_v.start()
+    own_out = remote(w_ref.at[:, own_cols], wbuf.at[own_rows], own_ss, own_rs, mate)
+    own_out.start()
+
+    def shard_rows(d, s, c):
+        place = (pos + (ring - s if d == 0 else s)) % ring
+        return pl.ds(pl.multiple_of((2 * chip_at(place) + c) * depth, 16), depth)
+
+    def used(d, s, q):
+        return s < far or (s == far and q == d)
+
+    def lanes(f, q):
+        off, w = pieces[f]
+        return pl.ds(off + q * w, w)
+
+    def ring_send(d, f, s, q):
+        off, w = pieces[f]
+        if s == 1:
+            src = w_ref.at[:, pl.ds(pl.multiple_of(col0 + off + q * w, 128), w)]
+            where = own_rows
+        else:
+            where = shard_rows(d, s - 1, core)
+            src = wbuf.at[where, lanes(f, q)]
+        return remote(
+            src, wbuf.at[where, lanes(f, q)], ring_ss.at[d, f, s - 1, q], ring_rs.at[d, f, s - 1, q],
+            nxt if d == 0 else prv,
+        )
+
+    def ring_recv(d, f, s, q):
+        here = wbuf.at[shard_rows(d, s, core), lanes(f, q)]
+        return remote(here, here, ring_ss.at[d, f, s - 1, q], ring_rs.at[d, f, s - 1, q], nxt)
+
+    def chip_copy(d, f, s, q, c):
+        here = wbuf.at[shard_rows(d, s, c), lanes(f, q)]
+        return remote(here, here, chip_ss.at[d, f, s - 1, q], chip_rs.at[d, f, s - 1, q], mate)
+
+    def launch(f):
+        for q in (0, 1):
+            for d in (0, 1):
+                if used(d, 1, q):
+                    ring_send(d, f, 1, q).start()
+
+    def ring_step(f, s):
+        for q in (0, 1):
+            for d in (0, 1):
+                if used(d, s, q):
+                    ring_recv(d, f, s, q).wait_recv()
+                    if s < far and used(d, s + 1, q):
+                        ring_send(d, f, s + 1, q).start()
+                    chip_copy(d, f, s, q, core).start()
+        if s == max(far - 1, 1) and f + 1 < len(pieces):
+            launch(f + 1)
+
+    launch(0)
+
+    def normed(x, gain):
+        x = x.astype(jnp.float32)
+        inverse = lax.rsqrt(jnp.mean(x * x, axis=-1, keepdims=True) + 1e-06)
+        return (x * inverse * gain).astype(jnp.bfloat16)
+
+    step_rows = 32
+
+    def normalise(src, src0, dst, dst0, gain):
+        @pl.loop(0, rows // step_rows)
+        def _(i):
+            x = src[pl.ds(pl.multiple_of(src0 + i * step_rows, 16), step_rows), :]
+            dst[pl.ds(pl.multiple_of(dst0 + i * step_rows, 16), step_rows), :] = normed(x, gain[...])
+
+    normalise(q_ref, 0, qn, 0, qg_ref)
+    normalise(k_ref, 0, kbuf, rows, kg_ref)
+
+    see_before = (reach_ref[0, 0] == 1) & not_first
+    see_after = (reach_ref[0, 1] == 1) & not_last
+    column = lax.broadcasted_iota(jnp.int32, (1, 3 * rows), 1)
+    lowest = jnp.where(see_before, 0, rows)
+    highest = jnp.where(see_after, 3 * rows, 2 * rows)
+    seen = (column >= lowest) & (column < highest)
+
+    def head(h):
+        at = pl.ds(pl.multiple_of(h * HD, 128), HD)
+        logits = lax.dot_general(
+            qn[:, at], kbuf[:, at], (((1,), (1,)), ((), ())), preferred_element_type=jnp.float32
+        ) * (HD ** (-0.5))
+        logits = jnp.where(seen, logits, -1e30)
+        top = jnp.max(logits, axis=-1, keepdims=True)
+        expo = jnp.exp(logits - top)
+        weights = (expo * (1.0 / jnp.sum(expo, axis=-1, keepdims=True))).astype(jnp.bfloat16)
+        att[0:rows, at] = jnp.dot(
+            weights, vbuf[:, at], preferred_element_type=jnp.float32
+        ).astype(jnp.bfloat16)
+
+    groups_of = 4 if heads % 4 == 0 else 1
+    per = heads // groups_of
+
+    def attention(i):
+        @pl.loop(0, per)
+        def _(j):
+            head(i * per + j)
+
+    def att_send(i):
+        at = pl.ds(i * per * HD, per * HD)
+        return remote(
+            att.at[pl.ds(0, rows), at], att.at[pl.ds(rows, rows), at], att_ss.at[i], att_rs.at[i], cross
+        )
+
+    def wait_halo():
+        local_v.wait()
+
+        @pl.when(not_first)
+        def _():
+            for c in halo(1):
+                c.wait_recv()
+            normalise(kbuf, 0, kbuf, 0, kg_ref)
+
+        @pl.when(t == 0)
+        def _():
+            kbuf[0:rows] = jnp.zeros((rows, chans), jnp.bfloat16)
+            vbuf[0:rows] = jnp.zeros((rows, chans), jnp.bfloat16)
+
+        @pl.when(not_last)
+        def _():
+            for c in halo(0):
+                c.wait_recv()
+            normalise(kbuf, 2 * rows, kbuf, 2 * rows, kg_ref)
+
+        @pl.when(t == tiles - 1)
+        def _():
+            kbuf[2 * rows : 3 * rows] = jnp.zeros((rows, chans), jnp.bfloat16)
+            vbuf[2 * rows : 3 * rows] = jnp.zeros((rows, chans), jnp.bfloat16)
+
+    def out_send(f):
+        off, w = pieces[f]
+        there = pl.ds(pl.multiple_of(col0 + off, 128), 2 * w)
+        return remote(
+            sbuf.at[:, pl.ds(off, 2 * w)], o_ref.at[:, there], out_ss.at[f], out_rs.at[f], cross
+        )
+
+    def out_recv(f):
+        off, w = pieces[f]
+        there = pl.ds(pl.multiple_of(half - col0 + off, 128), 2 * w)
+        return remote(o_ref.at[:, there], o_ref.at[:, there], out_ss.at[f], out_rs.at[f], cross)
+
+    def project(f):
+        off, w = pieces[f]
+        for s in range(1, far + 1):
+            for q in (0, 1):
+                for d in (0, 1):
+                    if used(d, s, q):
+                        chip_copy(d, f, s, q, 1 - core).wait_recv()
+        block = 256
+
+        @pl.loop(0, 2 * w // block)
+        def _(j):
+            at = pl.ds(pl.multiple_of(off + j * block, 128), block)
+            out_at = pl.ds(pl.multiple_of(col0 + off + j * block, 128), block)
+            total = jnp.dot(att[...], wbuf[:, at], preferred_element_type=jnp.float32)
+            scaled = (gate_ref[:, out_at] * total).astype(jnp.bfloat16)
+            sbuf[:, at] = scaled[rows:]
+            o_ref[:, out_at] = scaled[:rows]
+
+        out_send(f).start()
+
+    queue = [(f, s) for f in range(len(pieces)) for s in range(1, far + 1)]
+    ring_step(*queue.pop(0))
+    wait_halo()
+    for i in range(groups_of):
+        attention(i)
+        if i > 0:
+            att_send(i - 1).start()
+        if queue:
+            ring_step(*queue.pop(0))
+    att_send(groups_of - 1).start()
+    local_w.wait()
+    first_wait = True
+    todo = list(range(len(pieces)))
+    while todo:
+        f = todo[0]
+        while queue and (queue[0][0] <= f or (queue[0][0] == f + 1 and queue[0][1] <= min(2, far))):
+            ring_step(*queue.pop(0))
+        if first_wait:
+            remote(
+                w_ref.at[:, own_cols],
+                wbuf.at[pl.ds(pl.multiple_of((2 * chip + 1 - core) * depth, 16), depth)],
+                own_ss, own_rs, mate,
+            ).wait_recv()
+            for i in range(groups_of):
+                att_send(i).wait_recv()
+            first_wait = False
+        project(f)
+        todo.pop(0)
+
+    own_out.wait_send()
+
+    @pl.when(not_last)
+    def _():
+        for c in halo(1):
+            c.wait_send()
+
+    @pl.when(not_first)
+    def _():
+        for c in halo(0):
+            c.wait_send()
+
+    for i in range(groups_of):
+        att_send(i).wait_send()
+    for f in range(len(pieces)):
+        for s in range(1, far + 1):
+            for q in (0, 1):
+                for d in (0, 1):
+                    if used(d, s, q):
+                        ring_send(d, f, s, q).wait_send()
+                        chip_copy(d, f, s, q, core).wait_send()
+    for f in range(len(pieces)):
+        out_send(f).wait_send()
+        out_recv(f).wait_recv()
+
+
+def fused(peers, queries, keys, values, q_gain, k_gain, out_weight, out_gate, reach):
+    rows, chans = queries.shape
+    depth, wide = out_weight.shape
+    half = wide // 2
+    ring = peers // 2
+    far = ring // 2
+    parts = len(lane_pieces(half))
+    groups_of = 4 if (chans // HD) % 4 == 0 else 1
+    dma = pltpu.SemaphoreType.DMA
+    vmem = pl.BlockSpec(memory_space=pltpu.VMEM)
+    return pl.pallas_call(
+        functools.partial(fused_kernel, ring),
+        out_shape=jax.ShapeDtypeStruct((rows, wide), jnp.bfloat16),
+        in_specs=[vmem] * 7 + [pl.BlockSpec(memory_space=pltpu.SMEM)],
+        out_specs=vmem,
+        scratch_shapes=[
+            pltpu.VMEM((depth * peers, half), jnp.bfloat16),
+            pltpu.VMEM((3 * rows, chans), jnp.bfloat16),
+            pltpu.VMEM((3 * rows, chans), jnp.bfloat16),
+            pltpu.VMEM((rows, chans), jnp.bfloat16),
+            pltpu.VMEM((2 * rows, chans), jnp.bfloat16),
+            pltpu.VMEM((rows, half), jnp.bfloat16),
+            dma((2, parts, far, 2)),
+            dma((2, parts, far, 2)),
+            dma((2, parts, far, 2)),
+            dma((2, parts, far, 2)),
+            dma, dma,
+            dma((2, 2)), dma((2, 2)),
+            dma((groups_of,)), dma((groups_of,)),
+            dma((parts,)), dma((parts,)),
+            dma((2,)),
+        ],
+        compiler_params=pltpu.CompilerParams(
+            collective_id=0, has_side_effects=True, vmem_limit_bytes=60 * 1024 * 1024
+        ),
+    )(
+        queries, keys, values, q_gain.reshape(1, -1), k_gain.reshape(1, -1), out_weight,
+        out_gate.reshape(1, -1), reach,
+    )
+
+
 def solution(mesh):
+    groups, peers = mesh.shape["groups"], mesh.shape["tm"]
+
+    def step(queries, keys, values, q_gain, k_gain, out_weight, out_gate, reach):
+        fits = (
+            groups % 2 == 0
+            and peers % 8 == 0
+            and queries.shape[0] == TT * TH * TW
+            and out_weight.shape[0] % 16 == 0
+            and out_weight.shape[1] % 512 == 0
+        )
+        args = (queries, keys, values, q_gain, k_gain, out_weight, out_gate, reach)
+        return fused(peers, *args) if fits else local(*args)
+
     return jax.shard_map(
-        local,
+        step,
         mesh=mesh,
         in_specs=(
             P(("groups", "tm"), None),

time: 203 us -> 140 us (0.69)
  Pallas kernels: 0 us -> 132 us
  waiting for transfers between devices: 102 us -> 0 us
  matrix products: 24.2 us -> 0 us
  local copies, waits for them, and re-layouts: 28.6 us -> 5.57 us
  other arithmetic: 20.3 us -> 0 us
  between operations: 14.9 us -> 0.01 us
  starting transfers between devices: 11.1 us -> 0 us
    pallas_call x0 -> x1, Pallas kernels: none -> 132 us  [fused(): pl.pallas_call(functools.partial(fused_kernel, ring), out_shape=jax.Shape...]
    all_gather x1 -> x0, waiting for transfers between devices: 72.7 us -> none  [local(): full_weight = lax.all_gather(out_weight, 'tm', axis=0, tiled=True)]
    ppermute x4 -> x0, waiting for transfers between devices: 28.8 us -> none  [shifted(): return lax.ppermute(shard, axis, pairs)]
    dot_general x2 -> x0, matrix products: 18.1 us -> none  [the longest x1 12.7 us: local(): jnp.dot(attended, full_weight, preferred_element_type=jnp.float32)]
    another operation x10 -> x0, local copies, waits for them, and re-layouts: 12.3 us -> none  [the longest x6 6.58 us: local(): jnp.stack([key_buffer[offset:offset + count] for offset in range(3)], axi...]
    reduce_max x1 -> x0, other arithmetic: 12.2 us -> none  [local(): top = jnp.max(logits, axis=-1, keepdims=True)]
    ppermute x4 -> x0, starting transfers between devices: 11.1 us -> none  [shifted(): return lax.ppermute(shard, axis, pairs)]
    reshape x1 -> x2, local copies, waits for them, and re-layouts: 11.7 us -> 2.62 us  [the longest x1 1.31 us: fused(): q_gain.reshape(1, -1)]
  transfers between devices with their start and end apart: 5 -> 0, of which waited for: 3 -> 0; matrix products, arithmetic and copies ran while one was open for 28% -> 0% of each run, Pallas kernels for 0% -> 0%
where the time goes in v1:
time: 140 us; the launch traced here: 137 us
  Pallas kernels  132 us (94%)
  local copies, waits for them, and re-layouts  5.57 us (4%)
    pallas_call x1, Pallas kernels, fused(): pl.pallas_call(functools.partial(fused_kernel, ring), out_shape=jax.Shape...  132 us
    unnamed x1, local copies, waits for them, and re-layouts  2.94 us

profile of v1, /device:TPU:4, one launch (start us, length us, event | category | flops | bytes accessed | tf_op | source)
XLA Modules:
  0.0 137.3 jit_solution(9955299115830821781)
XLA Ops:
  0.0 1.3 reshape.9.qg_ref
  1.3 1.3 reshape.10.kg_ref
  2.6 131.8 %shard_map.82 = bf16[192,5120]{1,0:T(8,128)(2,1)} custom-call(bf16[192,2560]{1,0:T(8,128)(2,1)} %q_ref.1, bf16[192,2560]{1,0:T(8,128)(2,1)} %k_ref.1, bf16[192,2560]{1,0:T(8,128)(2,1)} %v_ref.1, f32[1,2560]{1,0:T(1,128)} %reshape.9.qg_ref, f32[1,2560]{1,0:T(1,128)} %reshape.10.kg_ref, bf16[160,5120]{1,0:T(8,128)(2,1)} %w_ref.1, f32[1,5120]{1,0:T(1,128)} %bitcast.1, ...), custom_call_target="tpu_custom_call" | custom-call | tf_op jit(solution)/shard_map/pallas_call | solution.py:398
  134.4 2.9 %copy.10 = bf16[192,5120]{1,0:T(8,128)(2,1)} copy(bf16[192,5120]{1,0:T(8,128)(2,1)} %shard_map.82) | data formatting | bytes 3932160

commit v2 on v1

--- a/solution.py
+++ b/solution.py
@@ -12,6 +12,7 @@
 TH = 6
 TW = 8
 MESH = pl.DeviceIdType.MESH
+SCHEDULE = ("H0", "L", "H1", "H2", "H3", "R", "Y0", "R", "Y1", "A", "R", "Y2", "A", "R", "Y3", "A", "R", "A", "R", "S", "R", "P", "R", "R", "P", "R", "R", "P")
 
 
 def shifted(shard, axis, by):
@@ -93,8 +94,8 @@
 
 def fused_kernel(
     ring, q_ref, k_ref, v_ref, qg_ref, kg_ref, w_ref, gate_ref, reach_ref, o_ref,
-    wbuf, kbuf, vbuf, qn, att, sbuf,
-    ring_ss, ring_rs, chip_ss, chip_rs, own_ss, own_rs, halo_ss, halo_rs,
+    wbuf, kbuf, vbuf, held, qn, att, sbuf,
+    ring_ss, ring_rs, chip_ss, chip_rs, own_ss, own_rs, mate_ss, mate_rs, side_ss, side_rs, relay_ss, relay_rs,
     att_ss, att_rs, out_ss, out_rs, local_sem,
 ):
     rows, chans = q_ref.shape
@@ -130,38 +131,126 @@
             src_ref=src, dst_ref=dst, send_sem=ss, recv_sem=rs, device_id=dev, device_id_type=MESH
         )
 
+    def normed(x, gain):
+        x = x.astype(jnp.float32)
+        inverse = lax.rsqrt(jnp.mean(x * x, axis=-1, keepdims=True) + 1e-06)
+        return (x * inverse * gain).astype(jnp.bfloat16)
+
+    step_rows = 32
+
+    def normalise(src, src0, dst, dst0, gain):
+        @pl.loop(0, rows // step_rows)
+        def _(i):
+            x = src[pl.ds(pl.multiple_of(src0 + i * step_rows, 16), step_rows), :]
+            dst[pl.ds(pl.multiple_of(dst0 + i * step_rows, 16), step_rows), :] = normed(x, gain[...])
+
+    normalise(q_ref, 0, qn, 0, qg_ref)
+    normalise(k_ref, 0, kbuf, rows, kg_ref)
+
     barrier = pltpu.get_barrier_semaphore()
     for dev in (nxt, prv, mate, cross):
         pl.semaphore_signal(barrier, inc=1, device_id=dev, device_id_type=MESH)
 
-    @pl.when(has_outside)
+    low, high = 4, 4 * (far - 1)
+    base = jnp.where(t <= low, 6, high - 4)
+    ends = (t == low) | (t == low - 1) | (t == high) | (t == high - 1)
+    relays = (t // 2 == 3) | (t // 2 == (high - 4) // 2)
+    served = jnp.where(t // 2 == 3, low - 1, high - 1)
+    direct = has_outside & jnp.logical_not(ends)
+
+    def greet(tm):
+        pl.semaphore_signal(barrier, inc=1, device_id=peer(g, tm), device_id_type=MESH)
+
+    pl.when(direct)(lambda: greet(outside))
+
+    @pl.when(ends)
     def _():
-        pl.semaphore_signal(barrier, inc=1, device_id=peer(g, outside), device_id_type=MESH)
-        pl.semaphore_wait(barrier, 5)
-
-    @pl.when(jnp.logical_not(has_outside))
+        greet(base)
+        greet(base + 1)
+
+    @pl.when(relays)
     def _():
-        pl.semaphore_wait(barrier, 4)
-
-    def halo(side):
-        to = peer(g, t + (1 if side else -1))
-        there = pl.ds((0 if side else 2) * rows, rows)
+        greet(served)
+        greet(served + 1)
+
+    plain = jnp.logical_not(relays)
+    pl.when(ends)(lambda: pl.semaphore_wait(barrier, 6))
+    pl.when(relays)(lambda: pl.semaphore_wait(barrier, 7))
+    pl.when(direct & plain)(lambda: pl.semaphore_wait(barrier, 5))
+    pl.when(jnp.logical_not(has_outside))(lambda: pl.semaphore_wait(barrier, 4))
+
+    def slot(number, start=0, size=rows):
+        return pl.ds(pl.multiple_of(number * rows + start, 16), size)
+
+    groups_of = 4 if heads % 4 == 0 else 1
+    per = heads // groups_of
+
+    def group_cols(i):
+        return pl.ds(i * per * HD, per * HD)
+
+    def pairs(i, number):
+        cols = group_cols(i)
+        return (
+            (kbuf.at[slot(1), cols], kbuf.at[slot(number), cols]),
+            (v_ref.at[:, cols], vbuf.at[slot(number), cols]),
+        )
+
+    def mate_halo(i, number):
         return [
-            remote(k_ref, kbuf.at[there], halo_ss.at[side, 0], halo_rs.at[side, 0], to),
-            remote(v_ref, vbuf.at[there], halo_ss.at[side, 1], halo_rs.at[side, 1], to),
+            remote(src, dst, mate_ss.at[i, n], mate_rs.at[i, n], mate)
+            for n, (src, dst) in enumerate(pairs(i, number))
         ]
 
-    not_first, not_last = t > 0, t < tiles - 1
-
-    @pl.when(not_last)
-    def _():
-        for c in halo(1):
+    for i in range(groups_of):
+        for c in mate_halo(i, 2 * core):
             c.start()
 
-    @pl.when(not_first)
-    def _():
-        for c in halo(0):
-            c.start()
+    def side_send(i):
+        return [
+            remote(src, dst, side_ss.at[i, n], side_rs.at[i, n], peer(g, outside))
+            for n, (src, dst) in enumerate(pairs(i, 2 * (1 - core)))
+        ]
+
+    def side_recv(i):
+        return [
+            remote(dst, dst, side_ss.at[i, n], side_rs.at[i, n], cross)
+            for n, (_, dst) in enumerate(pairs(i, 2 * core))
+        ]
+
+    def relay_in(i):
+        return [
+            remote(
+                src, held.at[n, :, group_cols(i)], side_ss.at[i, n], relay_rs.at[i, n], peer(g, base + core)
+            )
+            for n, (src, _) in enumerate(pairs(i, 1))
+        ]
+
+    def relay_out(i):
+        return [
+            remote(
+                held.at[n, :, group_cols(i)], dst, relay_ss.at[i, n], side_rs.at[i, n],
+                peer(g, served + core),
+            )
+            for n, (_, dst) in enumerate(pairs(i, 2 * (1 - core)))
+        ]
+
+    def halo_issue(i):
+        @pl.when(direct)
+        def _():
+            for c in side_send(i):
+                c.start()
+
+        @pl.when(ends)
+        def _():
+            for c in relay_in(i):
+                c.start()
+
+    def relay_step(i):
+        @pl.when(relays)
+        def _():
+            for c, d in zip(relay_in(i), relay_out(i)):
+                c.wait_recv()
+                d.start()
 
     own_rows = pl.ds(pl.multiple_of(t * depth, 16), depth)
     own_cols = pl.ds(pl.multiple_of(col0, 128), half)
@@ -221,26 +310,9 @@
         if s == max(far - 1, 1) and f + 1 < len(pieces):
             launch(f + 1)
 
-    launch(0)
-
-    def normed(x, gain):
-        x = x.astype(jnp.float32)
-        inverse = lax.rsqrt(jnp.mean(x * x, axis=-1, keepdims=True) + 1e-06)
-        return (x * inverse * gain).astype(jnp.bfloat16)
-
-    step_rows = 32
-
-    def normalise(src, src0, dst, dst0, gain):
-        @pl.loop(0, rows // step_rows)
-        def _(i):
-            x = src[pl.ds(pl.multiple_of(src0 + i * step_rows, 16), step_rows), :]
-            dst[pl.ds(pl.multiple_of(dst0 + i * step_rows, 16), step_rows), :] = normed(x, gain[...])
-
-    normalise(q_ref, 0, qn, 0, qg_ref)
-    normalise(k_ref, 0, kbuf, rows, kg_ref)
-
-    see_before = (reach_ref[0, 0] == 1) & not_first
-    see_after = (reach_ref[0, 1] == 1) & not_last
+
+    see_before = (reach_ref[0, 0] == 1) & (t > 0)
+    see_after = (reach_ref[0, 1] == 1) & (t < tiles - 1)
     column = lax.broadcasted_iota(jnp.int32, (1, 3 * rows), 1)
     lowest = jnp.where(see_before, 0, rows)
     highest = jnp.where(see_after, 3 * rows, 2 * rows)
@@ -259,9 +331,6 @@
             weights, vbuf[:, at], preferred_element_type=jnp.float32
         ).astype(jnp.bfloat16)
 
-    groups_of = 4 if heads % 4 == 0 else 1
-    per = heads // groups_of
-
     def attention(i):
         @pl.loop(0, per)
         def _(j):
@@ -273,30 +342,14 @@
             att.at[pl.ds(0, rows), at], att.at[pl.ds(rows, rows), at], att_ss.at[i], att_rs.at[i], cross
         )
 
-    def wait_halo():
-        local_v.wait()
-
-        @pl.when(not_first)
+    def wait_halo(i):
+        for c in mate_halo(i, 2 * (1 - core)):
+            c.wait_recv()
+
+        @pl.when(has_outside)
         def _():
-            for c in halo(1):
+            for c in side_recv(i):
                 c.wait_recv()
-            normalise(kbuf, 0, kbuf, 0, kg_ref)
-
-        @pl.when(t == 0)
-        def _():
-            kbuf[0:rows] = jnp.zeros((rows, chans), jnp.bfloat16)
-            vbuf[0:rows] = jnp.zeros((rows, chans), jnp.bfloat16)
-
-        @pl.when(not_last)
-        def _():
-            for c in halo(0):
-                c.wait_recv()
-            normalise(kbuf, 2 * rows, kbuf, 2 * rows, kg_ref)
-
-        @pl.when(t == tiles - 1)
-        def _():
-            kbuf[2 * rows : 3 * rows] = jnp.zeros((rows, chans), jnp.bfloat16)
-            vbuf[2 * rows : 3 * rows] = jnp.zeros((rows, chans), jnp.bfloat16)
 
     def out_send(f):
         off, w = pieces[f]
@@ -331,45 +384,62 @@
         out_send(f).start()
 
     queue = [(f, s) for f in range(len(pieces)) for s in range(1, far + 1)]
-    ring_step(*queue.pop(0))
-    wait_halo()
+    started = taken = 0
+    local_v.wait()
+
+    @pl.when(jnp.logical_not(has_outside))
+    def _():
+        kbuf[slot(2 * core)] = jnp.zeros((rows, chans), jnp.bfloat16)
+        vbuf[slot(2 * core)] = jnp.zeros((rows, chans), jnp.bfloat16)
+
+    for act in SCHEDULE:
+        if act == "L":
+            launch(0)
+        elif act == "R" and queue:
+            ring_step(*queue.pop(0))
+        elif act[0] == "H" and int(act[1]) < groups_of:
+            halo_issue(int(act[1]))
+        elif act[0] == "Y" and int(act[1]) < groups_of:
+            relay_step(int(act[1]))
+        elif act == "A" and taken < groups_of:
+            wait_halo(taken)
+            attention(taken)
+            if taken > 0:
+                att_send(taken - 1).start()
+            taken += 1
+        elif act == "S":
+            att_send(groups_of - 1).start()
+        elif act == "P" and started < len(pieces):
+            while queue and queue[0][0] <= started:
+                ring_step(*queue.pop(0))
+            if started == 0:
+                local_w.wait()
+                remote(
+                    w_ref.at[:, own_cols],
+                    wbuf.at[pl.ds(pl.multiple_of((2 * chip + 1 - core) * depth, 16), depth)],
+                    own_ss, own_rs, mate,
+                ).wait_recv()
+                for i in range(groups_of):
+                    att_send(i).wait_recv()
+            project(started)
+            started += 1
+
+    own_out.wait_send()
     for i in range(groups_of):
-        attention(i)
-        if i > 0:
-            att_send(i - 1).start()
-        if queue:
-            ring_step(*queue.pop(0))
-    att_send(groups_of - 1).start()
-    local_w.wait()
-    first_wait = True
-    todo = list(range(len(pieces)))
-    while todo:
-        f = todo[0]
-        while queue and (queue[0][0] <= f or (queue[0][0] == f + 1 and queue[0][1] <= min(2, far))):
-            ring_step(*queue.pop(0))
-        if first_wait:
-            remote(
-                w_ref.at[:, own_cols],
-                wbuf.at[pl.ds(pl.multiple_of((2 * chip + 1 - core) * depth, 16), depth)],
-                own_ss, own_rs, mate,
-            ).wait_recv()
-            for i in range(groups_of):
-                att_send(i).wait_recv()
-            first_wait = False
-        project(f)
-        todo.pop(0)
-
-    own_out.wait_send()
-
-    @pl.when(not_last)
+        for c in mate_halo(i, 2 * core):
+            c.wait_send()
+
+    @pl.when(has_outside)
     def _():
-        for c in halo(1):
-            c.wait_send()
-
-    @pl.when(not_first)
+        for i in range(groups_of):
+            for c in side_send(i):
+                c.wait_send()
+
+    @pl.when(relays)
     def _():
-        for c in halo(0):
-            c.wait_send()
+        for i in range(groups_of):
+            for c in relay_out(i):
+                c.wait_send()
 
     for i in range(groups_of):
         att_send(i).wait_send()
@@ -404,6 +474,7 @@
             pltpu.VMEM((depth * peers, half), jnp.bfloat16),
             pltpu.VMEM((3 * rows, chans), jnp.bfloat16),
             pltpu.VMEM((3 * rows, chans), jnp.bfloat16),
+            pltpu.VMEM((2, rows, chans), jnp.bfloat16),
             pltpu.VMEM((rows, chans), jnp.bfloat16),
             pltpu.VMEM((2 * rows, chans), jnp.bfloat16),
             pltpu.VMEM((rows, half), jnp.bfloat16),
@@ -412,7 +483,8 @@
             dma((2, parts, far, 2)),
             dma((2, parts, far, 2)),
             dma, dma,
-            dma((2, 2)), dma((2, 2)),
+            dma((groups_of, 2)), dma((groups_of, 2)), dma((groups_of, 2)), dma((groups_of, 2)),
+            dma((groups_of, 2)), dma((groups_of, 2)),
             dma((groups_of,)), dma((groups_of,)),
             dma((parts,)), dma((parts,)),
             dma((2,)),
@@ -432,7 +504,8 @@
     def step(queries, keys, values, q_gain, k_gain, out_weight, out_gate, reach):
         fits = (
             groups % 2 == 0
-            and peers % 8 == 0
+            and peers % 4 == 0
+            and peers >= 16
             and queries.shape[0] == TT * TH * TW
             and out_weight.shape[0] % 16 == 0
             and out_weight.shape[1] % 512 == 0

time: 140 us -> 132 us (0.943); the launches traced: 137 us -> 132 us
  Pallas kernels: 132 us -> 126 us
    pallas_call x1, Pallas kernels: 132 us -> 126 us  [fused(): pl.pallas_call(functools.partial(fused_kernel, ring), out_shape=jax.Shape...]
where the time goes in v2:
time: 132 us
  Pallas kernels  126 us (95%)
  local copies, waits for them, and re-layouts  5.57 us (4%)
    pallas_call x1, Pallas kernels, fused(): pl.pallas_call(functools.partial(fused_kernel, ring), out_shape=jax.Shape...  126 us
    unnamed x1, local copies, waits for them, and re-layouts  2.94 us

profile of v2, /device:TPU:4, one launch (start us, length us, event | category | flops | bytes accessed | tf_op | source)
XLA Modules:
  0.0 131.7 jit_solution(5468194498227357411)
XLA Ops:
  0.0 1.3 reshape.9.qg_ref
  1.3 1.3 reshape.10.kg_ref
  2.6 126.1 %shard_map.82 = bf16[192,5120]{1,0:T(8,128)(2,1)} custom-call(bf16[192,2560]{1,0:T(8,128)(2,1)} %q_ref.1, bf16[192,2560]{1,0:T(8,128)(2,1)} %k_ref.1, bf16[192,2560]{1,0:T(8,128)(2,1)} %v_ref.1, f32[1,2560]{1,0:T(1,128)} %reshape.9.qg_ref, f32[1,2560]{1,0:T(1,128)} %reshape.10.kg_ref, bf16[160,5120]{1,0:T(8,128)(2,1)} %w_ref.1, f32[1,5120]{1,0:T(1,128)} %bitcast.1, ...), custom_call_target="tpu_custom_call" | custom-call | tf_op jit(solution)/shard_map/pallas_call | solution.py:468
  128.7 2.9 %copy.10 = bf16[192,5120]{1,0:T(8,128)(2,1)} copy(bf16[192,5120]{1,0:T(8,128)(2,1)} %shard_map.82) | data formatting | bytes 3932160

commit v3 on v2

--- a/solution.py
+++ b/solution.py
@@ -142,7 +142,7 @@
         @pl.loop(0, rows // step_rows)
         def _(i):
             x = src[pl.ds(pl.multiple_of(src0 + i * step_rows, 16), step_rows), :]
-            dst[pl.ds(pl.multiple_of(dst0 + i * step_rows, 16), step_rows), :] = normed(x, gain[...])
+            dst[pl.ds(pl.multiple_of(dst0 + i * step_rows, 16), step_rows), :] = normed(x, gain[...].reshape(1, -1))
 
     normalise(q_ref, 0, qn, 0, qg_ref)
     normalise(k_ref, 0, kbuf, rows, kg_ref)
@@ -493,7 +493,7 @@
             collective_id=0, has_side_effects=True, vmem_limit_bytes=60 * 1024 * 1024
         ),
     )(
-        queries, keys, values, q_gain.reshape(1, -1), k_gain.reshape(1, -1), out_weight,
+        queries, keys, values, q_gain, k_gain, out_weight,
         out_gate.reshape(1, -1), reach,
     )
 

time: 132 us -> 129 us (0.977)
  local copies, waits for them, and re-layouts: 5.57 us -> 2.94 us
    reshape x2 -> x0, local copies, waits for them, and re-layouts: 2.62 us -> none  [the longest x1 1.31 us: fused(): q_gain.reshape(1, -1)]
where the time goes in v3:
time: 129 us
  Pallas kernels  126 us (98%)
  local copies, waits for them, and re-layouts  2.94 us (2%)
    pallas_call x1, Pallas kernels, fused(): pl.pallas_call(functools.partial(fused_kernel, ring), out_shape=jax.Shape...  126 us
    unnamed x1, local copies, waits for them, and re-layouts  2.94 us

profile of v3, /device:TPU:4, one launch (start us, length us, event | category | flops | bytes accessed | tf_op | source)
XLA Modules:
  0.0 129.0 jit_solution(1195239533125818284)
XLA Ops:
  0.0 126.1 %shard_map.82 = bf16[192,5120]{1,0:T(8,128)(2,1)} custom-call(bf16[192,2560]{1,0:T(8,128)(2,1)} %q_ref.1, bf16[192,2560]{1,0:T(8,128)(2,1)} %k_ref.1, bf16[192,2560]{1,0:T(8,128)(2,1)} %v_ref.1, f32[2560]{0:T(1024)} %qg_ref.1, f32[2560]{0:T(1024)} %kg_ref.1, bf16[160,5120]{1,0:T(8,128)(2,1)} %w_ref.1, f32[1,5120]{1,0:T(1,128)} %bitcast.1, s32[1,2]{1,0:T(1,128)} %reach_ref.1), custom_call_target="tpu_custom_call" | custom-call | tf_op jit(solution)/shard_map/pallas_call | solution.py:468
  126.1 2.9 %copy.10 = bf16[192,5120]{1,0:T(8,128)(2,1)} copy(bf16[192,5120]{1,0:T(8,128)(2,1)} %shard_map.82) | data formatting | bytes 3932160
